TPU v7x, 32 devices: a whole 2x2x4 slice. The times are simulated.
32 devices in a mesh: grp: 2 (over y), row: 8 (over z, x), col: 2 (over core).
Axes of the slice: x: 2, y: 2, z: 4, core: 2. Of those that a mesh axis runs over, the one named last changes fastest.
Arguments:
- grad_out: bfloat16 [1024, 8192], P(('grp', 'row'), 'col'), parts along dimension 0, may hold values from -6 to 6
- hidden_act: bfloat16 [1024, 22016], P(('grp', 'col'), 'row'), parts along dimension 0, may hold values from -6 to 6
- down_weight: bfloat16 [22016, 8192], P('row', 'col'), may hold values from -0.0390625 to 0.0390625
- proj_in: bfloat16 [22016, 64], P('row'), may hold values from -0.0390625 to 0.0390625
- proj_out: bfloat16 [8192, 64], P('col'), may hold values from -0.0625 to 0.0625
- queries: bfloat16 [128, 4096], P('row', 'col'), may hold values from -0.01171875 to 0.01171875
- example_ids: int32 [1024], P(('grp', 'row')), parts along dimension 0, may hold values from 0 to 7, never falling along the last dimension, each value on 1 to 128 neighbouring positions
Outputs:
- grad_hidden: bfloat16 [1024, 22016], P(('grp', 'col'), 'row'), parts along dimension 0
- weight_grad: bfloat16 [44032, 8192], P(('grp', 'row'), 'col'), parts along dimension 0
- scores: float32 [128, 16], P(('row', 'col'), 'grp'), parts along dimension 1
There are 2 independent parts, one for each index of `grp`. A program takes and returns all parts, laid end to end along the dimension named above; an argument that names none is the same for every part. Nothing has to cross between parts.
Inputs may be any that keep to these rules, and one draw needn't show every extreme that they name: `example_ids`: never falling along the tokens; each example holds 1 to 128 tokens, one exactly 128.
All inputs are finite; a program needn't handle non-finite values.
Results may differ from a plain program's by a relative error of at most 0.001.
Values may be sent and summed in bfloat16 or wider, within the bound.
A program may use at most 192 MiB of HBM per device.

v0:
```python
import jax
import jax.numpy as jnp
from jax import lax
from jax.sharding import PartitionSpec as P

EXAMPLES = 8


def body(grad_out, hidden_act, down_weight, proj_in, proj_out, queries, example_ids):
    full_hidden = lax.all_gather(hidden_act, "col", axis=0, tiled=True)
    full_grad = lax.all_gather(grad_out, "row", axis=0, tiled=True)
    token_rows = full_grad
    grad_hidden = lax.psum_scatter(
        lax.dot_general(
            token_rows, down_weight, (((1,), (1,)), ((), ())), preferred_element_type=jnp.float32
        ),
        "col",
        scatter_dimension=0,
        tiled=True,
    ).astype(jnp.bfloat16)
    weight_grad = lax.dot_general(
        full_hidden, full_grad, (((0,), (0,)), ((), ())), preferred_element_type=jnp.float32
    ).astype(jnp.bfloat16)
    token_rows = full_hidden
    in_factor = lax.psum_scatter(
        jnp.dot(token_rows, proj_in, preferred_element_type=jnp.float32),
        "row",
        scatter_dimension=0,
        tiled=True,
    )
    out_factor = lax.psum(jnp.dot(grad_out, proj_out, preferred_element_type=jnp.float32), "col")
    split_rank = in_factor.shape[1] // lax.axis_size("col")
    own_factor = lax.dynamic_slice_in_dim(
        in_factor, lax.axis_index("col") * split_rank, split_rank, 1
    )
    outer_terms = (own_factor[:, :, None] * out_factor[:, None, :]).reshape(own_factor.shape[0], -1)
    labels = jnp.arange(EXAMPLES, dtype=jnp.int32)
    onehot = (example_ids[None, :] == labels[:, None]).astype(jnp.float32)
    partial_grads = jnp.dot(onehot, outer_terms, precision=lax.Precision.HIGHEST)
    example_grads = lax.psum(partial_grads, "row")
    values = jnp.dot(queries.astype(jnp.float32), example_grads.T, precision=lax.Precision.HIGHEST)
    scores = lax.psum_scatter(values, "col", scatter_dimension=0, tiled=True)
    return (grad_hidden, weight_grad, scores)


def solution(mesh):
    return jax.shard_map(
        body,
        mesh=mesh,
        in_specs=(
            P(("grp", "row"), "col"),
            P(("grp", "col"), "row"),
            P("row", "col"),
            P("row", None),
            P("col", None),
            P("row", "col"),
            P(("grp", "row")),
        ),
        out_specs=(P(("grp", "col"), "row"), P(("grp", "row"), "col"), P(("row", "col"), "grp")),
        check_vma=False,
    )
```

profile of v0, /device:TPU:0, one launch (start us, length us, event | category | flops | bytes accessed | tf_op | source)
XLA Modules:
  0.0 267.6 jit_solution(11298728215527538428)
XLA Ops:
  7.2 0.0 copy-start
  7.2 0.0 copy-start.1
  7.2 0.0 all-gather.5.cloned.1.call-start
  7.2 0.7 all-gather.5.cloned.1.call-update
  7.9 0.0 copy-start.3
  7.9 0.0 reduce-scatter.6.cloned.1.call-start
  8.0 15.3 %all-gather.5.cloned.1.call-done = bf16[512,2752]{0,1:T(8,128)(2,1)} async-done(((bf16[256,2752]{0,1:T(8,128)(2,1)}), bf16[512,2752]{0,1:T(8,128)(2,1)}) %all-gather.5.cloned.1.call-update) | async-done | bytes 2818064 | tf_op jit(solution)/shard_map/all_gather | solution.py:10
  23.3 3.5 %fusion.3 = f32[512,64]{1,0:T(8,128)} fusion(bf16[512,2752]{0,1:T(8,128)(2,1)} %all-gather.5.cloned.1.call-done, bf16[2752,64]{0,1:T(8,128)(2,1)} %param.10), kind=kOutput, calls=%fused_computation.9 | convolution fusion | flops 180355072 | bytes 3301376 | tf_op jit(solution)/shard_map/dot_general | solution.py:26
  26.8 0.0 reduce-scatter.6.cloned.1.call-update
  26.8 0.0 all-gather.3.cloned.1.call-start
  26.9 0.7 all-gather.3.cloned.1.call-update
  27.6 0.0 all-reduce.3.cloned.1.call-start
  27.6 0.0 copy-done
  27.6 0.0 copy-done.1
  27.6 0.3 fusion.4
  27.9 3.5 %psum.14 = f32[64,64]{1,0:T(8,128)S(1)} all-reduce(f32[64,64]{1,0:T(8,128)S(1)} %fusion.4), channel_id=1, replica_groups=mesh['grp'=2,'row'=8,'col'=2] {'col'}, use_global_device_ids=true, to_apply=%region_2.0 | all-reduce | flops 4096 | bytes 32768 | tf_op jit(solution)/shard_map/psum | solution.py:31
  31.4 59.1 %reduce-scatter.6.cloned.1.call-done = f32[64,64]{1,0:T(8,128)} async-done(((f32[512,64]{1,0:T(8,128)}), f32[64,64]{1,0:T(8,128)}) %reduce-scatter.6.cloned.1.call-update) | async-done | bytes 16400 | tf_op jit(solution)/shard_map/reduce_scatter | solution.py:25
  90.5 0.8 constant_dynamic-slice_fusion.1
  91.3 0.3 broadcast_multiply_fusion
  91.7 0.4 mul.24
  92.1 0.0 copy-done.3
  92.1 0.9 fusion
  93.0 0.0 all-reduce.3.cloned.1.call-update
  93.0 0.0 reduce-scatter.4.cloned.1.call-start
  93.1 71.5 %all-gather.3.cloned.1.call-done = bf16[512,4096]{1,0:T(8,128)(2,1)} async-done(((bf16[64,4096]{1,0:T(8,128)(2,1)}), bf16[512,4096]{1,0:T(8,128)(2,1)}) %all-gather.3.cloned.1.call-update) | async-done | bytes 4194320 | tf_op jit(solution)/shard_map/all_gather | solution.py:11
  164.5 19.1 %fusion.2 = f32[512,2752]{0,1:T(8,128)} fusion(bf16[512,4096]{1,0:T(8,128)(2,1)} %all-gather.3.cloned.1.call-done, bf16[2752,4096]{1,0:T(8,128)(2,1)} %param.9), kind=kOutput, calls=%fused_computation.8 | convolution fusion | flops 11542724608 | bytes 32374784 | tf_op jit(solution)/shard_map/dot_general | solution.py:14
  183.6 0.0 copy-start.5
  183.6 0.0 copy-start.2
  183.6 0.0 copy-start.4
  183.6 0.0 reduce-scatter.4.cloned.1.call-update
  183.7 0.6 copy-done.5
  184.3 0.6 dynamic-slice
  185.5 50.7 %all-reduce.3.cloned.1.call-done = f32[8,2048]{1,0:T(8,128)} async-done(((f32[8,2048]{1,0:T(8,128)}), f32[8,2048]{1,0:T(8,128)}) %all-reduce.3.cloned.1.call-update) | async-done | bytes 65552 | tf_op jit(solution)/shard_map/psum | solution.py:40
  236.2 0.0 copy-done.2
  236.2 1.0 convolution_bitcast_fusion
  237.2 2.5 all-reduce
  239.7 0.1 constant_dynamic-slice_fusion
  239.8 0.7 copy.11
  240.5 0.0 copy-done.4
  240.5 17.6 %convolution_convert_fusion = bf16[2752,4096]{1,0:T(8,128)(2,1)} fusion(bf16[512,2752]{0,1:T(8,128)(2,1)S(1)} %copy-done.4, bf16[512,4096]{1,0:T(8,128)(2,1)} %all-gather.3.cloned.1.call-done), kind=kOutput, calls=%fused_computation | convolution fusion | flops 11553996800 | bytes 29556736 | tf_op jit(solution)/shard_map/dot_general | solution.py:21
  258.0 0.0 reduce-scatter.4.cloned.1.call-done
  258.0 3.0 %convert_element_type.8 = bf16[256,2752]{0,1:T(8,128)(2,1)} convert(f32[256,2752]{0,1:T(8,128)} %reduce-scatter.4.cloned.1.call-done) | non-fusion elementwise | flops 704512 | bytes 4227072 | tf_op jit(solution)/shard_map/convert_element_type | solution.py:20
Async XLA Ops:
  7.2 20.5 %copy-start = (bf16[4096,64]{0,1:T(8,128)(2,1)S(1)}, bf16[4096,64]{0,1:T(8,128)(2,1)}, u32[]{:S(2)}) copy-start(bf16[4096,64]{0,1:T(8,128)(2,1)} %param.11) | copy-start | bytes 1572868
  7.2 20.4 %copy-start.1 = (bf16[64,4096]{1,0:T(8,128)(2,1)S(1)}, bf16[64,4096]{1,0:T(8,128)(2,1)}, u32[]{:S(2)}) copy-start(bf16[64,4096]{1,0:T(8,128)(2,1)} %param.7) | copy-start | bytes 1572868
  7.2 16.1 %all-gather.5.cloned.1.call-start = ((), (), s32[]{:S(2)}) async-start(), calls=%async_computation.4 | async-start | bytes 4227072 | tf_op jit(solution)/shard_map/all_gather | solution.py:10
  7.9 84.1 %copy-start.3 = (s32[64]{0:T(128)S(1)}, s32[64]{0:T(128)}, u32[]{:S(2)}) copy-start(s32[64]{0:T(128)} %param.13) | copy-start | bytes 772
  7.9 82.6 %reduce-scatter.6.cloned.1.call-start = ((), (), s32[]{:S(2)}) async-start(), calls=%async_computation.5 | async-start | bytes 294912 | tf_op jit(solution)/shard_map/reduce_scatter | solution.py:25
  26.8 137.7 %all-gather.3.cloned.1.call-start = ((), (), s32[]{:S(2)}) async-start(), calls=%async_computation.2 | async-start | bytes 4718592 | tf_op jit(solution)/shard_map/all_gather | solution.py:11
  27.6 208.7 %all-reduce.3.cloned.1.call-start = ((), (), s32[]{:S(2)}) async-start(), calls=%async_computation.6 | async-start | bytes 131072 | tf_op jit(solution)/shard_map/psum | solution.py:40
  93.0 165.0 %reduce-scatter.4.cloned.1.call-start = ((), (), s32[]{:S(2)}) async-start(), calls=%async_computation.3 | async-start | bytes 8454144 | tf_op jit(solution)/shard_map/reduce_scatter | solution.py:13
  183.6 0.7 copy-start.5
  183.6 52.6 %copy-start.2 = (bf16[16,2048]{1,0:T(8,128)(2,1)S(1)}, bf16[16,2048]{1,0:T(8,128)(2,1)}, u32[]{:S(2)}) copy-start(bf16[16,2048]{1,0:T(8,128)(2,1)} %param.12) | copy-start | bytes 196612
  183.6 56.8 %copy-start.4 = (bf16[512,2752]{0,1:T(8,128)(2,1)S(1)}, bf16[512,2752]{0,1:T(8,128)(2,1)}, u32[]{:S(2)}) copy-start(bf16[512,2752]{0,1:T(8,128)(2,1)} %all-gather.5.cloned.1.call-done) | copy-start | bytes 8454148
Sparse Core Ops, SparseCore 0:
  9.5 13.7 all-gather.4
  27.2 63.2 reduce-scatter.5
  92.6 71.8 all-gather.2
  168.4 67.8 all-reduce.2
  238.4 13.1 reduce-scatter.3
where the time goes:
time: 268 us
  waiting for transfers between devices  198 us (74%)
  matrix products  42.3 us (16%)
  between operations  14.5 us (5%)
  blocking collectives  5.99 us (2%)
  other arithmetic  3.36 us (1%)
  local copies, waits for them, and re-layouts  3.16 us (1%)
    all_gather x1, waiting for transfers between devices, body(): full_grad = lax.all_gather(grad_out, 'row', axis=0, tiled=True)  71.5 us
    reduce_scatter x1, waiting for transfers between devices, body(): lax.psum_scatter(jnp.dot(token_rows, proj_in, preferred_element_type=jnp....  59.1 us
    psum x1, waiting for transfers between devices, body(): example_grads = lax.psum(partial_grads, 'row')  50.7 us
    dot_general x1, matrix products, body(): lax.dot_general(token_rows, down_weight, (((1,), (1,)), ((), ())), prefer...  19.1 us
    dot_general x1, matrix products, body(): lax.dot_general(full_hidden, full_grad, (((0,), (0,)), ((), ())), preferr...  17.6 us
    all_gather x1, waiting for transfers between devices, body(): full_hidden = lax.all_gather(hidden_act, 'col', axis=0, tiled=True)  15.3 us
  transfers between devices with their start and end apart: 5, of which 4 were waited for; matrix products, arithmetic and copies ran while one was open for 16% of the time, Pallas kernels for 0%

commit v1 on v0

--- a/solution.py
+++ b/solution.py
@@ -37,7 +37,11 @@
     labels = jnp.arange(EXAMPLES, dtype=jnp.int32)
     onehot = (example_ids[None, :] == labels[:, None]).astype(jnp.float32)
     partial_grads = jnp.dot(onehot, outer_terms, precision=lax.Precision.HIGHEST)
-    example_grads = lax.psum(partial_grads, "row")
+    example_grads = partial_grads
+    for hop in (1, 2, 4):
+        example_grads = example_grads + lax.ppermute(
+            example_grads, "row", [(dev, dev ^ hop) for dev in range(8)]
+        )
     values = jnp.dot(queries.astype(jnp.float32), example_grads.T, precision=lax.Precision.HIGHEST)
     scores = lax.psum_scatter(values, "col", scatter_dimension=0, tiled=True)
     return (grad_hidden, weight_grad, scores)

time: 268 us -> 213 us (0.79)
  waiting for transfers between devices: 198 us -> 139 us
  starting transfers between devices: 0.2 us -> 4.64 us
    psum x1 -> x0, waiting for transfers between devices: 50.7 us -> none  [body(): example_grads = lax.psum(partial_grads, 'row')]
    reduce_scatter x1, waiting for transfers between devices: 59.1 us -> 40.6 us  [body(): lax.psum_scatter(jnp.dot(token_rows, proj_in, preferred_element_type=jnp....]
    ppermute x0 -> x3, waiting for transfers between devices: none -> 9.57 us  [body(): lax.ppermute(example_grads, 'row', [(dev, dev ^ hop) for dev in range(8)])]
    ppermute x0 -> x3, starting transfers between devices: none -> 4.48 us  [body(): lax.ppermute(example_grads, 'row', [(dev, dev ^ hop) for dev in range(8)])]
  transfers between devices with their start and end apart: 5 -> 7, of which waited for: 4 -> 6; matrix products, arithmetic and copies ran while one was open for 16% -> 21% of each run, Pallas kernels for 0% -> 0%
where the time goes in v1:
time: 213 us
  waiting for transfers between devices  139 us (65%)
  matrix products  42.2 us (20%)
  between operations  14.5 us (7%)
  blocking collectives  5.91 us (3%)
  starting transfers between devices  4.64 us (2%)
  local copies, waits for them, and re-layouts  3.52 us (2%)
  other arithmetic  3.38 us (2%)
    all_gather x1, waiting for transfers between devices, body(): full_grad = lax.all_gather(grad_out, 'row', axis=0, tiled=True)  72.6 us
    reduce_scatter x1, waiting for transfers between devices, body(): lax.psum_scatter(jnp.dot(token_rows, proj_in, preferred_element_type=jnp....  40.6 us
    dot_general x1, matrix products, body(): lax.dot_general(token_rows, down_weight, (((1,), (1,)), ((), ())), prefer...  19.1 us
    dot_general x1, matrix products, body(): lax.dot_general(full_hidden, full_grad, (((0,), (0,)), ((), ())), preferr...  18.9 us
    all_gather x1, waiting for transfers between devices, body(): full_hidden = lax.all_gather(hidden_act, 'col', axis=0, tiled=True)  14.6 us
    ppermute x3, waiting for transfers between devices, body(): lax.ppermute(example_grads, 'row', [(dev, dev ^ hop) for dev in range(8)])  9.57 us
    ppermute x3, starting transfers between devices, body(): lax.ppermute(example_grads, 'row', [(dev, dev ^ hop) for dev in range(8)])  4.48 us
  transfers between devices with their start and end apart: 7, of which 6 were waited for; matrix products, arithmetic and copies ran while one was open for 21% of the time, Pallas kernels for 0%

profile of v1, /device:TPU:0, one launch (start us, length us, event | category | flops | bytes accessed | tf_op | source)
XLA Modules:
  0.0 213.0 jit_solution(15309762173657897590)
XLA Ops:
  7.2 0.0 copy-start
  7.2 0.0 all-gather.5.cloned.1.call-start
  7.2 0.7 all-gather.5.cloned.1.call-update
  7.9 0.0 all-gather.3.cloned.1.call-start
  8.0 0.7 all-gather.3.cloned.1.call-update
  8.7 0.0 reduce-scatter.6.cloned.1.call-start
  8.7 14.6 %all-gather.5.cloned.1.call-done = bf16[512,2752]{0,1:T(8,128)(2,1)} async-done(((bf16[256,2752]{0,1:T(8,128)(2,1)}), bf16[512,2752]{0,1:T(8,128)(2,1)}) %all-gather.5.cloned.1.call-update) | async-done | bytes 2818064 | tf_op jit(solution)/shard_map/all_gather | solution.py:10
  23.3 3.5 %fusion.4 = f32[512,64]{1,0:T(8,128)} fusion(bf16[512,2752]{0,1:T(8,128)(2,1)} %all-gather.5.cloned.1.call-done, bf16[2752,64]{0,1:T(8,128)(2,1)} %param.10), kind=kOutput, calls=%fused_computation.10 | convolution fusion | flops 180355072 | bytes 3301376 | tf_op jit(solution)/shard_map/dot_general | solution.py:26
  26.8 0.0 reduce-scatter.6.cloned.1.call-update
  26.8 0.0 reduce-scatter.4.cloned.1.call-start
  26.9 72.6 %all-gather.3.cloned.1.call-done = bf16[512,4096]{1,0:T(8,128)(2,1)} async-done(((bf16[64,4096]{1,0:T(8,128)(2,1)}), bf16[512,4096]{1,0:T(8,128)(2,1)}) %all-gather.3.cloned.1.call-update) | async-done | bytes 4194320 | tf_op jit(solution)/shard_map/all_gather | solution.py:11
  99.5 19.1 %fusion.3 = f32[512,2752]{0,1:T(8,128)} fusion(bf16[512,4096]{1,0:T(8,128)(2,1)} %all-gather.3.cloned.1.call-done, bf16[2752,4096]{1,0:T(8,128)(2,1)} %param.9), kind=kOutput, calls=%fused_computation.9 | convolution fusion | flops 11542724608 | bytes 32374784 | tf_op jit(solution)/shard_map/dot_general | solution.py:14
  118.5 0.0 copy-start.2
  118.5 0.0 copy-start.4
  118.5 0.0 copy-start.5
  118.5 0.0 copy-start.3
  118.6 0.0 reduce-scatter.4.cloned.1.call-update
  118.6 0.0 copy-done
  118.6 1.0 copy-done.2
  119.6 0.3 fusion.5
  119.9 3.4 %psum.7 = f32[64,64]{1,0:T(8,128)S(1)} all-reduce(f32[64,64]{1,0:T(8,128)S(1)} %fusion.5), channel_id=1, replica_groups=mesh['grp'=2,'row'=8,'col'=2] {'col'}, use_global_device_ids=true, to_apply=%region_2.0 | all-reduce | flops 4096 | bytes 32768 | tf_op jit(solution)/shard_map/psum | solution.py:31
  123.3 40.6 %reduce-scatter.6.cloned.1.call-done = f32[64,64]{1,0:T(8,128)} async-done(((f32[512,64]{1,0:T(8,128)}), f32[64,64]{1,0:T(8,128)}) %reduce-scatter.6.cloned.1.call-update) | async-done | bytes 16400 | tf_op jit(solution)/shard_map/reduce_scatter | solution.py:25
  164.0 0.8 constant_dynamic-slice_fusion.1
  164.8 0.3 broadcast_multiply_fusion
  165.2 0.4 mul.24
  165.5 0.0 copy-done.4
  165.5 0.3 fusion.1
  165.8 1.5 collective-permute-start
  167.3 2.8 %collective-permute-done = f32[8,2048]{1,0:T(8,128)S(1)} collective-permute-done((f32[8,2048]{1,0:T(8,128)S(1)}, f32[8,2048]{1,0:T(8,128)S(1)}, u32[]{:S(2)}, u32[]{:S(2)}) %collective-permute-start) | collective-permute-done | bytes 65568 | tf_op jit(solution)/shard_map/ppermute | solution.py:42
  170.2 1.5 collective-permute-start.1
  171.7 3.5 %collective-permute-done.1 = f32[8,2048]{1,0:T(8,128)S(1)} collective-permute-done((f32[8,2048]{1,0:T(8,128)S(1)}, f32[8,2048]{1,0:T(8,128)S(1)}, u32[]{:S(2)}, u32[]{:S(2)}) %collective-permute-start.1) | collective-permute-done | bytes 65568 | tf_op jit(solution)/shard_map/ppermute | solution.py:42
  175.2 1.5 collective-permute-start.2
  176.7 0.0 copy-done.5
  176.7 0.6 dynamic-slice
  177.9 3.2 %collective-permute-done.2 = f32[8,2048]{1,0:T(8,128)S(1)} collective-permute-done((f32[8,2048]{1,0:T(8,128)S(1)}, f32[8,2048]{1,0:T(8,128)S(1)}, u32[]{:S(2)}, u32[]{:S(2)}) %collective-permute-start.2) | collective-permute-done | bytes 65568 | tf_op jit(solution)/shard_map/ppermute | solution.py:42
  181.1 0.0 copy-done.3
  181.1 0.1 convolution_bitcast_fusion
  181.3 2.5 %all-reduce = f32[16,8]{0,1:T(8,128)S(1)} all-reduce(f32[16,8]{0,1:T(8,128)S(1)} %convolution_bitcast_fusion), channel_id=4, replica_groups=mesh['grp'=2,'row'=8,'col'=2] {'col'}, use_global_device_ids=true, to_apply=%region_3.0.clone | all-reduce | flops 128 | bytes 1024
  183.8 0.1 constant_dynamic-slice_fusion
  183.8 0.7 copy.11
  184.5 0.0 copy-start.1
  184.5 18.9 %convolution_convert_fusion = bf16[2752,4096]{1,0:T(8,128)(2,1)} fusion(bf16[512,2752]{0,1:T(8,128)(2,1)} %all-gather.5.cloned.1.call-done, bf16[512,4096]{1,0:T(8,128)(2,1)} %all-gather.3.cloned.1.call-done), kind=kOutput, calls=%fused_computation | convolution fusion | flops 11553996800 | bytes 29556736 | tf_op jit(solution)/shard_map/dot_general | solution.py:21
  203.4 0.0 reduce-scatter.4.cloned.1.call-done
  203.4 3.0 %convert_element_type.8 = bf16[256,2752]{0,1:T(8,128)(2,1)} convert(f32[256,2752]{0,1:T(8,128)} %reduce-scatter.4.cloned.1.call-done) | non-fusion elementwise | flops 704512 | bytes 4227072 | tf_op jit(solution)/shard_map/convert_element_type | solution.py:20
  206.4 0.0 copy-done.1
  (2 shorter events, 0.0 us)
Async XLA Ops:
  7.2 111.4 %copy-start = (bf16[4096,64]{0,1:T(8,128)(2,1)S(1)}, bf16[4096,64]{0,1:T(8,128)(2,1)}, u32[]{:S(2)}) copy-start(bf16[4096,64]{0,1:T(8,128)(2,1)} %param.11) | copy-start | bytes 1572868
  7.2 16.1 %all-gather.5.cloned.1.call-start = ((), (), s32[]{:S(2)}) async-start(), calls=%async_computation.4 | async-start | bytes 4227072 | tf_op jit(solution)/shard_map/all_gather | solution.py:10
  7.9 91.5 %all-gather.3.cloned.1.call-start = ((), (), s32[]{:S(2)}) async-start(), calls=%async_computation.2 | async-start | bytes 4718592 | tf_op jit(solution)/shard_map/all_gather | solution.py:11
  8.7 155.3 %reduce-scatter.6.cloned.1.call-start = ((), (), s32[]{:S(2)}) async-start(), calls=%async_computation.5 | async-start | bytes 294912 | tf_op jit(solution)/shard_map/reduce_scatter | solution.py:25
  26.8 176.6 %reduce-scatter.4.cloned.1.call-start = ((), (), s32[]{:S(2)}) async-start(), calls=%async_computation.3 | async-start | bytes 8454144 | tf_op jit(solution)/shard_map/reduce_scatter | solution.py:13
  118.5 1.0 copy-start.2
  118.5 47.0 %copy-start.4 = (s32[64]{0:T(128)S(1)}, s32[64]{0:T(128)}, u32[]{:S(2)}) copy-start(s32[64]{0:T(128)} %param.13) | copy-start | bytes 772
  118.5 58.1 %copy-start.5 = (u32[32]{0:T(128)S(1)}, u32[32]{0:T(128)}, u32[]{:S(2)}) copy-start(u32[32]{0:T(128)} %constant.12) | copy-start | bytes 388
  118.5 62.6 %copy-start.3 = (bf16[16,2048]{1,0:T(8,128)(2,1)S(1)}, bf16[16,2048]{1,0:T(8,128)(2,1)}, u32[]{:S(2)}) copy-start(bf16[16,2048]{1,0:T(8,128)(2,1)} %param.12) | copy-start | bytes 196612
  165.8 4.3 %collective-permute-start = (f32[8,2048]{1,0:T(8,128)S(1)}, f32[8,2048]{1,0:T(8,128)S(1)}, u32[]{:S(2)}, u32[]{:S(2)}) collective-permute-start(f32[8,2048]{1,0:T(8,128)S(1)} %fusion.1), channel_id=1, source_target_pairs={{0,2},{2,0},{4,6},{6,4},{8,10},{10,8},{12,14},{14,12},{1,3},{3,1},... | collective-permute-start | bytes 196616 | tf_op jit(solution)/shard_map/ppermute | solution.py:42
  170.2 5.0 %collective-permute-start.1 = (f32[8,2048]{1,0:T(8,128)S(1)}, f32[8,2048]{1,0:T(8,128)S(1)}, u32[]{:S(2)}, u32[]{:S(2)}) collective-permute-start(f32[8,2048]{1,0:T(8,128)S(1)} %add.21), channel_id=1, source_target_pairs={{0,4},{2,6},{4,0},{6,2},{8,12},{10,14},{12,8},{14,10},{1,5},{3,7},... | collective-permute-start | bytes 196616 | tf_op jit(solution)/shard_map/ppermute | solution.py:42
  175.2 5.9 %collective-permute-start.2 = (f32[8,2048]{1,0:T(8,128)S(1)}, f32[8,2048]{1,0:T(8,128)S(1)}, u32[]{:S(2)}, u32[]{:S(2)}) collective-permute-start(f32[8,2048]{1,0:T(8,128)S(1)} %add.22), channel_id=1, source_target_pairs={{0,8},{2,10},{4,12},{6,14},{8,0},{10,2},{12,4},{14,6},{1,9},{3,11}... | collective-permute-start | bytes 196616 | tf_op jit(solution)/shard_map/ppermute | solution.py:42
  184.5 21.9 %copy-start.1 = (bf16[4096,64]{0,1:T(8,128)(2,1)S(1)}, bf16[4096,64]{0,1:T(8,128)(2,1)}, u32[]{:S(2)}) copy-start(bf16[4096,64]{0,1:T(8,128)(2,1)} %param.11) | copy-start | bytes 1572868
Sparse Core Ops, SparseCore 0:
  9.5 13.7 all-gather.4
  25.4 73.9 all-gather.2
  103.4 60.5 reduce-scatter.5
  166.1 12.2 reduce-scatter.3
